TPU v7x, 512 devices: a whole 4x8x8 slice. The times are simulated.
512 devices in a mesh: fsdp: 128 (over z, y, core), seq: 4 (over x).
Axes of the slice: x: 4, y: 8, z: 8, core: 2. Of those that a mesh axis runs over, the one named last changes fastest.
Arguments:
- text_embeds: bfloat16 [35840, 4096], P('fsdp'), may hold values from -8 to 8
- vision_tokens: bfloat16 [16384, 4096], P('fsdp', 'seq'), may hold values from -6 to 6
- vision_request: int32 [16384, 1], P('fsdp'), may hold values from 0 to 127; in each aligned block of 128 rows (0 to 127, 128 to 255, ...) at most 2 rows name the same one
- image_start: int32 [128], P('fsdp'), may hold values from 1 to 16
- lengths: int32 [128], P('fsdp'), may hold values from 273 to 280
- attn_gain: float32 [4096], replicated, may hold values from 0.5 to 1.5
- w_query: bfloat16 [4096, 2048], P('fsdp', 'seq'), may hold values from -1 to 1
- w_key: bfloat16 [4096, 2048], P('fsdp', 'seq'), may hold values from -1 to 1
- w_value: bfloat16 [4096, 2048], P('fsdp', 'seq'), may hold values from -0.09375 to 0.09375
- w_out: bfloat16 [2048, 4096], P(None, 'fsdp'), may hold values from -0.125 to 0.125
- final_gain: float32 [4096], replicated, may hold values from 0.25 to 1.75
- lm_head: bfloat16 [4096, 32000], P(None, 'fsdp'), may hold values from -0.25 to 0.25
Outputs:
- state_rms: float32 [128], P('seq')
- max_logit: float32 [128], P('seq')
Inputs may be any that keep to these rules, and one draw needn't show every extreme that they name: `vision_request`: within the 128 vision tokens of one index of fsdp no request is named more than 2 times, a bound that some block reaches; every request is named by some vision token. `lengths`: each request's image tokens end before its last token.
All inputs are finite; a program needn't handle non-finite values.
Results may differ from a plain program's by a relative error of at most 0.0024.
Values may be sent and summed in bfloat16 or wider, within the bound.
No kernel may reach another device: no remote copies, remote signals or barrier semaphores. Data moves between devices by JAX's collectives and lax.ppermute only.
A program may use at most 128 MiB of HBM per device.

v0:
```python
import math
import jax
import jax.numpy as jnp
from jax import lax
from jax.sharding import PartitionSpec as P

HD = 128
norm_epsilon = 1e-05


def row_norm(rows, gain):
    widened = rows.astype(jnp.float32)
    return (
        widened
        * lax.rsqrt(jnp.mean(widened * widened, axis=1, keepdims=True) + norm_epsilon)
        * gain
    ).astype(jnp.bfloat16)


def exchange(rows, axis_name):
    return lax.all_to_all(rows, axis_name, split_axis=0, concat_axis=0, tiled=True)


def gather_by_exchange(piece, axis_name, count):
    spread = jnp.broadcast_to(piece[None], (count,) + piece.shape)
    return exchange(spread, axis_name)


def select_rows(selector, rows):
    return jnp.dot(selector.astype(jnp.bfloat16), rows, preferred_element_type=jnp.float32).astype(
        jnp.bfloat16
    )


def local(
    text_embeds,
    vision_tokens,
    vision_request,
    image_start,
    lengths,
    attn_gain,
    w_query,
    w_key,
    w_value,
    w_out,
    final_gain,
    lm_head,
):
    groups = lax.axis_size("fsdp")
    seq_count = lax.axis_size("seq")
    seq_index = lax.axis_index("seq")
    seq_len = text_embeds.shape[0]
    width = text_embeds.shape[1]
    columns = w_key.shape[1]
    heads_local = columns // HD
    dpiece = width // groups
    quarter = groups // seq_count
    capacity = max(2, 2 * vision_tokens.shape[0] // groups)
    last_index = lengths[0] - 1
    destination = vision_request[:, 0]
    onehot = (destination[:, None] == jnp.arange(groups, dtype=jnp.int32)[None, :]).astype(
        jnp.int32
    )
    slot_index = jnp.sum((jnp.cumsum(onehot, axis=0) - onehot) * onehot, axis=1)
    counts = jnp.sum(onehot, axis=0)
    final_text = lax.dynamic_slice_in_dim(text_embeds, last_index, 1, 0)
    last_normed = row_norm(final_text, attn_gain)
    pieces = jnp.stack(
        [
            final_text.reshape(groups, dpiece),
            last_normed.reshape(groups, dpiece),
            jnp.broadcast_to(counts.astype(jnp.bfloat16)[:, None], (groups, dpiece)),
        ],
        axis=1,
    )
    pieces_in = exchange(pieces, "fsdp")
    text_part = pieces_in[:, 0]
    normed_part = pieces_in[:, 1]
    arrived = pieces_in[:, 2, :1].astype(jnp.int32)
    query_partial = jnp.dot(normed_part, w_query, preferred_element_type=jnp.float32)
    query_all = lax.psum(query_partial, "fsdp").astype(jnp.bfloat16)
    query_heads = query_all.astype(jnp.float32).reshape(groups, heads_local, HD)
    key_rows = w_key.astype(jnp.float32).reshape(dpiece, heads_local, HD)
    probe_part = jnp.einsum("rhc,dhc->rhd", query_heads, key_rows, precision=lax.Precision.HIGHEST)
    probe_in = exchange(probe_part, "fsdp")
    probe = jnp.transpose(probe_in, (1, 0, 2)).reshape(heads_local, width)
    full_vision = lax.all_gather(vision_tokens, "seq", axis=1, tiled=True)
    slot_of = destination * capacity + slot_index
    outbox_select = jnp.arange(groups * capacity, dtype=jnp.int32)[:, None] == slot_of[None, :]
    outbox = select_rows(outbox_select, full_vision).reshape(groups, capacity, width)
    received = exchange(outbox, "fsdp")
    occupied = (
        (jnp.arange(capacity, dtype=jnp.int32)[None, :] < arrived).astype(jnp.int32).reshape(-1)
    )
    ranking = jnp.cumsum(occupied) - occupied
    positions = jnp.where(occupied > 0, image_start[0] + ranking, seq_len)
    place = jnp.arange(seq_len, dtype=jnp.int32)[:, None] == positions[None, :]
    placed = select_rows(place, received.reshape(-1, width))
    replaced = jnp.any(place, axis=1, keepdims=True)
    states = jnp.where(replaced, placed, text_embeds)
    normed = row_norm(states, attn_gain)
    scores = jnp.dot(
        normed.astype(jnp.float32), probe.T, precision=lax.Precision.HIGHEST
    ).T / math.sqrt(HD)
    live_keys = jnp.arange(seq_len, dtype=jnp.int32) < lengths[0]
    scores = jnp.where(live_keys[None, :], scores, -jnp.inf)
    peak = jnp.max(scores, axis=1, keepdims=True)
    shifted = jnp.exp(scores - peak)
    weights = (shifted / jnp.sum(shifted, axis=1, keepdims=True)).astype(jnp.bfloat16)
    mixed = jnp.dot(weights, normed, preferred_element_type=jnp.float32)
    mixed_pieces = jnp.transpose(mixed.reshape(heads_local, groups, dpiece), (1, 0, 2))
    mixed_in = exchange(mixed_pieces, "fsdp")
    value_rows = w_value.astype(jnp.float32).reshape(dpiece, heads_local, HD)
    attended_partial = jnp.einsum(
        "rhd,dhc->rhc", mixed_in, value_rows, precision=lax.Precision.HIGHEST
    ).reshape(groups, columns)
    attended_seq = lax.psum(attended_partial, "fsdp").astype(jnp.bfloat16)
    out_rows = lax.dynamic_slice_in_dim(w_out, seq_index * columns, columns, 0)
    partial_out = jnp.dot(attended_seq, out_rows, preferred_element_type=jnp.float32)
    out_mine = lax.psum_scatter(partial_out, "seq", scatter_dimension=0, tiled=True)
    text_mine = lax.dynamic_slice_in_dim(text_part, seq_index * quarter, quarter, 0)
    residual_out = text_mine.astype(jnp.float32) + out_mine
    residual_all = gather_by_exchange(residual_out, "fsdp", groups)
    last_state = jnp.transpose(residual_all, (1, 0, 2)).reshape(quarter, width)
    mean_square = jnp.mean(last_state * last_state, axis=1)
    scaled_out = (last_state * final_gain[None, :]).astype(jnp.bfloat16)
    logits = jnp.dot(scaled_out, lm_head, preferred_element_type=jnp.float32)
    local_max = jnp.max(logits, axis=1) * lax.rsqrt(mean_square + norm_epsilon)
    max_all = gather_by_exchange(local_max, "fsdp", groups)
    max_logit = jnp.max(max_all, axis=0)
    return (jnp.sqrt(mean_square), max_logit)


def solution(mesh):
    return jax.shard_map(
        local,
        mesh=mesh,
        in_specs=(
            P("fsdp", None),
            P("fsdp", "seq"),
            P("fsdp", None),
            P("fsdp"),
            P("fsdp"),
            P(),
            P("fsdp", "seq"),
            P("fsdp", "seq"),
            P("fsdp", "seq"),
            P(None, "fsdp"),
            P(),
            P(None, "fsdp"),
        ),
        out_specs=(P("seq"), P("seq")),
        check_vma=False,
    )
```

profile of v0, /device:TPU:1, one launch (start us, length us, event | category | flops | bytes accessed | tf_op | source)
XLA Modules:
  0.0 1239.9 jit_solution(17929459743585523007)
XLA Ops:
  14.5 18.4 %all-to-all-start = ((bf16[128,3,32]{2,1,0:T(4,128)(2,1)}), bf16[128,3,32]{2,1,0:T(4,128)(2,1)S(1)}, u32[]{:S(2)}, u32[]{:S(2)}) async-start(bf16[128,3,32]{2,1,0:T(4,128)(2,1)} %copy.59), calls=%async_computation | async-start | bytes 262144 | tf_op jit(solution)/shard_map/all_to_all | solution.py:21
  33.6 12.1 all-to-all-done
  46.8 485.9 %all-reduce.2 = bf16[128,512]{1,0:T(8,128)(2,1)S(1)} all-reduce(f32[128,512]{1,0:T(8,128)S(1)} %fusion.27), channel_id=1, replica_groups=mesh['fsdp'=128,'seq'=4] {'fsdp'}, use_global_device_ids=true, to_apply=%region_2.3 | all-reduce | flops 65536 | bytes 393216 | tf_op jit(solution)/shard_map/psum | solution.py:81
  533.8 11.7 all-to-all-start.1
  545.6 3.2 convolution_convert_fusion.1
  548.8 4.4 reshape.146
  553.2 3.8 all-to-all-done.1
  557.0 10.4 all-to-all-start.2
  568.2 2.4 fusion.17
  573.6 44.7 %all-to-all-done.2 = bf16[128,2,4096]{2,1,0:T(2,128)(2,1)} async-done(((bf16[128,2,4096]{2,1,0:T(2,128)(2,1)}), bf16[128,2,4096]{2,1,0:T(2,128)(2,1)}, u32[]{:S(2)}, u32[]{:S(2)}) %all-to-all-start.2) | async-done | bytes 2097184 | tf_op jit(solution)/shard_map/all_to_all | solution.py:21
  618.3 4.1 reshape.147
  622.4 3.3 fusion.1
  625.8 2.1 fusion.36
  630.0 8.9 all-to-all-start.3
  639.0 11.4 all-to-all-done.3
  651.8 486.1 %all-reduce.3 = bf16[128,512]{0,1:T(8,128)(2,1)S(1)} all-reduce(f32[128,512]{0,1:T(8,128)S(1)} %bitcast.64), channel_id=1, replica_groups=mesh['fsdp'=128,'seq'=4] {'fsdp'}, use_global_device_ids=true, to_apply=%region_11.12 | all-reduce | flops 65536 | bytes 393216 | tf_op jit(solution)/shard_map/psum | solution.py:117
  1139.5 22.1 %reduce-scatter.2.cloned.1.call-done = f32[32,32]{1,0:T(8,128)} async-done(((f32[128,32]{1,0:T(8,128)}), f32[32,32]{1,0:T(8,128)}) %reduce-scatter.2.cloned.1.call-update) | async-done | bytes 4112 | tf_op jit(solution)/shard_map/reduce_scatter | solution.py:120
  1164.0 2.5 reshape.165
  1166.5 36.9 %all_to_all.31 = f32[128,1,1024]{2,1,0:T(1,128)S(1)} all-to-all(f32[128,1,1024]{2,1,0:T(1,128)S(1)} %reshape.165), channel_id=1, replica_groups=mesh['fsdp'=128,'seq'=4] {'fsdp'}, dimensions={0} | all-to-all | bytes 1048576 | tf_op jit(solution)/shard_map/all_to_all | solution.py:21
  1205.3 2.0 reshape.166
  1207.3 2.1 multiply_reduce_fusion
  1209.5 2.6 copy.69
  1212.1 2.6 reshape.151
  1215.8 16.7 %all_to_all.32 = f32[128,1,32]{2,1,0:T(1,128)S(1)} all-to-all(f32[128,1,32]{2,1,0:T(1,128)S(1)} %broadcast_in_dim.36), channel_id=1, replica_groups=mesh['fsdp'=128,'seq'=4] {'fsdp'}, dimensions={0} | all-to-all | bytes 32768 | tf_op jit(solution)/shard_map/all_to_all | solution.py:21
  (73 shorter events, 23.3 us)
Async XLA Ops:
  7.2 1207.5 %copy-start = (bf16[4096,250]{1,0:T(8,128)(2,1)S(1)}, bf16[4096,250]{1,0:T(8,128)(2,1)}, u32[]{:S(2)}) copy-start(bf16[4096,250]{1,0:T(8,128)(2,1)} %param.23) | copy-start | bytes 6144004
  7.2 525.5 %copy-start.2 = (bf16[32,512]{1,0:T(8,128)(2,1)S(1)}, bf16[32,512]{1,0:T(8,128)(2,1)}, u32[]{:S(2)}) copy-start(bf16[32,512]{1,0:T(8,128)(2,1)} %param.19) | copy-start | bytes 98308
  7.2 538.4 %all-gather.2.cloned.1.call-start = ((), (), s32[]{:S(2)}) async-start(), calls=%async_computation.7 | async-start | bytes 1310720 | tf_op jit(solution)/shard_map/all_gather | solution.py:87
  14.5 31.2 %all-to-all-start = ((bf16[128,3,32]{2,1,0:T(4,128)(2,1)}), bf16[128,3,32]{2,1,0:T(4,128)(2,1)S(1)}, u32[]{:S(2)}, u32[]{:S(2)}) async-start(bf16[128,3,32]{2,1,0:T(4,128)(2,1)} %copy.59), calls=%async_computation | async-start | bytes 262144 | tf_op jit(solution)/shard_map/all_to_all | solution.py:21
  533.8 23.2 %all-to-all-start.1 = ((f32[128,1,128]{2,1,0:T(1,128)}), f32[128,1,128]{2,1,0:T(1,128)S(1)}, u32[]{:S(2)}, u32[]{:S(2)}) async-start(f32[128,1,128]{2,1,0:T(1,128)} %reshape.161), calls=%async_computation.1 | async-start | bytes 131072 | tf_op jit(solution)/shard_map/all_to_all | solution.py:21
  557.0 61.3 %all-to-all-start.2 = ((bf16[128,2,4096]{2,1,0:T(2,128)(2,1)}), bf16[128,2,4096]{2,1,0:T(2,128)(2,1)}, u32[]{:S(2)}, u32[]{:S(2)}) async-start(bf16[128,2,4096]{2,1,0:T(2,128)(2,1)} %reshape.146), calls=%async_computation.2 | async-start | bytes 4194304 | tf_op jit(solution)/shard_map/all_to_all | solution.py:21
  622.4 3.4 copy-start.5
  628.1 23.3 %copy-start.3 = (bf16[32,512]{1,0:T(8,128)(2,1)S(1)}, bf16[32,512]{1,0:T(8,128)(2,1)}, u32[]{:S(2)}) copy-start(bf16[32,512]{1,0:T(8,128)(2,1)} %param.20) | copy-start | bytes 98308
  630.0 20.4 %all-to-all-start.3 = ((f32[128,1,128]{2,1,0:T(1,128)}), f32[128,1,128]{2,1,0:T(1,128)S(1)}, u32[]{:S(2)}, u32[]{:S(2)}) async-start(f32[128,1,128]{2,1,0:T(1,128)} %reshape.163), calls=%async_computation.3 | async-start | bytes 131072 | tf_op jit(solution)/shard_map/all_to_all | solution.py:21
  639.0 522.7 %reduce-scatter.2.cloned.1.call-start = ((), (), s32[]{:S(2)}) async-start(), calls=%async_computation.8 | async-start | bytes 81920 | tf_op jit(solution)/shard_map/reduce_scatter | solution.py:120
  1207.3 2.2 copy-start.1
  1212.1 2.6 copy-start.4
Sparse Core Ops, SparseCore 0:
  10.1 33.8 all-gather.1
  1139.6 21.9 reduce-scatter.1
where the time goes:
time: 1240 us
  blocking collectives  1030 us (83%)
  waiting for transfers between devices  94.8 us (8%)
  starting transfers between devices  49.6 us (4%)
  local copies, waits for them, and re-layouts  25.1 us (2%)
  between operations  16.3 us (1%)
  other arithmetic  15.6 us (1%)
  matrix products  13.1 us (1%)
    psum x1, blocking collectives, local(): attended_seq = lax.psum(attended_partial, 'fsdp').astype(jnp.bfloat16)  486 us
    psum x1, blocking collectives, local(): query_all = lax.psum(query_partial, 'fsdp').astype(jnp.bfloat16)  486 us
    all_to_all x4, waiting for transfers between devices, exchange(): lax.all_to_all(rows, axis_name, split_axis=0, concat_axis=0, tiled=True)  72 us
    all_to_all x2, blocking collectives, exchange(): lax.all_to_all(rows, axis_name, split_axis=0, concat_axis=0, tiled=True)  53.6 us
    all_to_all x4, starting transfers between devices, exchange(): lax.all_to_all(rows, axis_name, split_axis=0, concat_axis=0, tiled=True)  49.5 us
  transfers between devices with their start and end apart: 6, of which 5 were waited for; matrix products, arithmetic and copies ran while one was open for 2% of the time, Pallas kernels for 0%

commit v1 on v0

--- a/solution.py
+++ b/solution.py
@@ -6,6 +6,12 @@
 
 HD = 128
 norm_epsilon = 1e-05
+
+
+def gather_and_add(x, name):
+    parts = lax.all_gather(x, name, axis=0, tiled=False)
+    total = parts.sum(axis=0)
+    return total
 
 
 def row_norm(rows, gain):
@@ -78,7 +84,7 @@
     normed_part = pieces_in[:, 1]
     arrived = pieces_in[:, 2, :1].astype(jnp.int32)
     query_partial = jnp.dot(normed_part, w_query, preferred_element_type=jnp.float32)
-    query_all = lax.psum(query_partial, "fsdp").astype(jnp.bfloat16)
+    query_all = gather_and_add(query_partial, "fsdp").astype(jnp.bfloat16)
     query_heads = query_all.astype(jnp.float32).reshape(groups, heads_local, HD)
     key_rows = w_key.astype(jnp.float32).reshape(dpiece, heads_local, HD)
     probe_part = jnp.einsum("rhc,dhc->rhd", query_heads, key_rows, precision=lax.Precision.HIGHEST)

time: 1240 us -> 879 us (0.71)
  blocking collectives: 1030 us -> 571 us
  waiting for transfers between devices: 94.8 us -> 194 us
  starting transfers between devices: 49.6 us -> 29.2 us
    psum x1 -> x0, blocking collectives: 486 us -> none  [local(): query_all = lax.psum(query_partial, 'fsdp').astype(jnp.bfloat16)]
    all_gather x0 -> x1, waiting for transfers between devices: none -> 96.5 us  [gather_and_add(): parts = lax.all_gather(x, name, axis=0, tiled=False)]
    all_to_all x2 -> x3, blocking collectives: 53.6 us -> 84.5 us  [exchange(): lax.all_to_all(rows, axis_name, split_axis=0, concat_axis=0, tiled=True)]
    all_to_all x4 -> x3, starting transfers between devices: 49.5 us -> 29.1 us  [exchange(): lax.all_to_all(rows, axis_name, split_axis=0, concat_axis=0, tiled=True)]
    all_to_all x4 -> x3, waiting for transfers between devices: 72 us -> 74.8 us  [exchange(): lax.all_to_all(rows, axis_name, split_axis=0, concat_axis=0, tiled=True)]
  transfers between devices with their start and end apart: 6 -> 6, of which waited for: 5 -> 5; matrix products, arithmetic and copies ran while one was open for 2% -> 3% of each run, Pallas kernels for 0% -> 0%
where the time goes in v1:
time: 879 us; the launch traced here: 878 us
  blocking collectives  571 us (65%)
  waiting for transfers between devices  194 us (22%)
  starting transfers between devices  29.2 us (3%)
  other arithmetic  26.9 us (3%)
  local copies, waits for them, and re-layouts  24.5 us (3%)
  matrix products  16.9 us (2%)
  between operations  16.1 us (2%)
    psum x1, blocking collectives, local(): attended_seq = lax.psum(attended_partial, 'fsdp').astype(jnp.bfloat16)  486 us
    all_gather x1, waiting for transfers between devices, gather_and_add(): parts = lax.all_gather(x, name, axis=0, tiled=False)  96.5 us
    all_to_all x3, blocking collectives, exchange(): lax.all_to_all(rows, axis_name, split_axis=0, concat_axis=0, tiled=True)  84.5 us
    all_to_all x3, waiting for transfers between devices, exchange(): lax.all_to_all(rows, axis_name, split_axis=0, concat_axis=0, tiled=True)  74.8 us
    all_to_all x3, starting transfers between devices, exchange(): lax.all_to_all(rows, axis_name, split_axis=0, concat_axis=0, tiled=True)  29.1 us
    reduce_scatter x1, waiting for transfers between devices, local(): lax.psum_scatter(partial_out, 'seq', scatter_dimension=0, tiled=True)  22 us
  transfers between devices with their start and end apart: 6, of which 5 were waited for; matrix products, arithmetic and copies ran while one was open for 3% of the time, Pallas kernels for 0%

profile of v1, /device:TPU:1, one launch (start us, length us, event | category | flops | bytes accessed | tf_op | source)
XLA Modules:
  0.0 878.3 jit_solution(13817283674888543951)
XLA Ops:
  13.9 31.0 %all_to_all.31 = bf16[128,3,32]{2,1,0:T(4,128)(2,1)S(1)} all-to-all(bf16[128,3,32]{2,1,0:T(4,128)(2,1)S(1)} %copy.61), channel_id=1, replica_groups=mesh['fsdp'=128,'seq'=4] {'fsdp'}, dimensions={0} | all-to-all | bytes 49152 | tf_op jit(solution)/shard_map/all_to_all | solution.py:27
  46.8 3.2 convolution_convert_fusion.1
  50.0 4.4 reshape.145
  54.5 12.9 %all-to-all-start.2 = ((bf16[128,2,4096]{2,1,0:T(2,128)(2,1)}), bf16[128,2,4096]{2,1,0:T(2,128)(2,1)}, u32[]{:S(2)}, u32[]{:S(2)}) async-start(bf16[128,2,4096]{2,1,0:T(2,128)(2,1)} %reshape.145), calls=%async_computation.2 | async-start | bytes 4194304 | tf_op jit(solution)/shard_map/all_to_all | solution.py:27
  68.2 2.4 fusion.15
  71.8 51.9 %all-to-all-done.2 = bf16[128,2,4096]{2,1,0:T(2,128)(2,1)} async-done(((bf16[128,2,4096]{2,1,0:T(2,128)(2,1)}), bf16[128,2,4096]{2,1,0:T(2,128)(2,1)}, u32[]{:S(2)}, u32[]{:S(2)}) %all-to-all-start.2) | async-done | bytes 2097184 | tf_op jit(solution)/shard_map/all_to_all | solution.py:27
  123.7 4.1 reshape.146
  127.8 4.6 fusion.1
  132.5 96.5 %all-gather.6.cloned.1.call-done = f32[16384,512]{1,0:T(8,128)} async-done(((f32[128,512]{1,0:T(8,128)}), f32[16384,512]{1,0:T(8,128)}) %all-gather.6.cloned.1.call-update) | async-done | bytes 33554448 | tf_op jit(solution)/shard_map/all_gather | solution.py:12
  228.9 12.0 %reduce_sum.65 = bf16[128,512]{1,0:T(8,128)(2,1)S(1)} reduce(f32[128,128,512]{2,1,0:T(8,128)} %bitcast.55, f32[]{:T(128)} %constant.19.clone.1), dimensions={0}, to_apply=%region_2.3 | reduce | flops 8323072 | bytes 33685508 | tf_op jit(solution)/shard_map/reduce_sum | solution.py:13
  242.2 10.5 %all-to-all-start.1 = ((f32[128,1,128]{2,1,0:T(1,128)}), f32[128,1,128]{2,1,0:T(1,128)S(1)}, u32[]{:S(2)}, u32[]{:S(2)}) async-start(f32[128,1,128]{2,1,0:T(1,128)} %reshape.161), calls=%async_computation.1 | async-start | bytes 131072 | tf_op jit(solution)/shard_map/all_to_all | solution.py:27
  252.7 11.4 %all-to-all-done.1 = f32[128,1,128]{2,1,0:T(1,128)S(1)} async-done(((f32[128,1,128]{2,1,0:T(1,128)}), f32[128,1,128]{2,1,0:T(1,128)S(1)}, u32[]{:S(2)}, u32[]{:S(2)}) %all-to-all-start.1) | async-done | bytes 65568 | tf_op jit(solution)/shard_map/all_to_all | solution.py:27
  265.8 3.9 fusion.34
  271.8 5.8 all-to-all-start.3
  277.6 11.5 %all-to-all-done.3 = f32[128,1,128]{2,1,0:T(1,128)S(1)} async-done(((f32[128,1,128]{2,1,0:T(1,128)}), f32[128,1,128]{2,1,0:T(1,128)S(1)}, u32[]{:S(2)}, u32[]{:S(2)}) %all-to-all-start.3) | async-done | bytes 65568 | tf_op jit(solution)/shard_map/all_to_all | solution.py:27
  290.6 486.1 %all-reduce.1 = bf16[128,512]{0,1:T(8,128)(2,1)S(1)} all-reduce(f32[128,512]{0,1:T(8,128)S(1)} %bitcast.59), channel_id=1, replica_groups=mesh['fsdp'=128,'seq'=4] {'fsdp'}, use_global_device_ids=true, to_apply=%region_11.12 | all-reduce | flops 65536 | bytes 393216 | tf_op jit(solution)/shard_map/psum | solution.py:123
  778.3 22.0 %reduce-scatter.2.cloned.1.call-done = f32[32,32]{1,0:T(8,128)} async-done(((f32[128,32]{1,0:T(8,128)}), f32[32,32]{1,0:T(8,128)}) %reduce-scatter.2.cloned.1.call-update) | async-done | bytes 4112 | tf_op jit(solution)/shard_map/reduce_scatter | solution.py:126
  802.7 2.5 reshape.165
  805.2 36.9 %all_to_all.32 = f32[128,1,1024]{2,1,0:T(1,128)S(1)} all-to-all(f32[128,1,1024]{2,1,0:T(1,128)S(1)} %reshape.165), channel_id=1, replica_groups=mesh['fsdp'=128,'seq'=4] {'fsdp'}, dimensions={0} | all-to-all | bytes 1048576 | tf_op jit(solution)/shard_map/all_to_all | solution.py:27
  843.9 2.0 reshape.166
  846.0 2.1 multiply_reduce_fusion
  848.2 2.6 copy.72
  850.8 2.6 reshape.150
  854.5 16.7 %all_to_all.33 = f32[128,1,32]{2,1,0:T(1,128)S(1)} all-to-all(f32[128,1,32]{2,1,0:T(1,128)S(1)} %broadcast_in_dim.36), channel_id=1, replica_groups=mesh['fsdp'=128,'seq'=4] {'fsdp'}, dimensions={0} | all-to-all | bytes 32768 | tf_op jit(solution)/shard_map/all_to_all | solution.py:27
  (80 shorter events, 22.8 us)
Async XLA Ops:
  7.2 846.2 %copy-start = (bf16[4096,250]{1,0:T(8,128)(2,1)S(1)}, bf16[4096,250]{1,0:T(8,128)(2,1)}, u32[]{:S(2)}) copy-start(bf16[4096,250]{1,0:T(8,128)(2,1)} %param.23) | copy-start | bytes 6144004
  7.2 39.6 %copy-start.6 = (s32[128,1]{0,1:T(1,128)S(1)}, s32[128,1]{0,1:T(1,128)}, u32[]{:S(2)}) copy-start(s32[128,1]{0,1:T(1,128)} %param.14) | copy-start | bytes 1540
  7.2 39.6 %all-gather.4.cloned.1.call-start = ((), (), s32[]{:S(2)}) async-start(), calls=%async_computation.7 | async-start | bytes 1310720 | tf_op jit(solution)/shard_map/all_gather | solution.py:93
  7.9 221.0 %all-gather.6.cloned.1.call-start = ((), (), s32[]{:S(2)}) async-start(), calls=%async_computation.9 | async-start | bytes 33816576 | tf_op jit(solution)/shard_map/all_gather | solution.py:12
  54.5 69.3 %all-to-all-start.2 = ((bf16[128,2,4096]{2,1,0:T(2,128)(2,1)}), bf16[128,2,4096]{2,1,0:T(2,128)(2,1)}, u32[]{:S(2)}, u32[]{:S(2)}) async-start(bf16[128,2,4096]{2,1,0:T(2,128)(2,1)} %reshape.145), calls=%async_computation.2 | async-start | bytes 4194304 | tf_op jit(solution)/shard_map/all_to_all | solution.py:27
  228.9 12.1 %copy-start.2 = (bf16[32,512]{1,0:T(8,128)(2,1)S(1)}, bf16[32,512]{1,0:T(8,128)(2,1)}, u32[]{:S(2)}) copy-start(bf16[32,512]{1,0:T(8,128)(2,1)} %param.19) | copy-start | bytes 98308
  240.9 24.9 %copy-start.5 = (f32[4096]{0:T(1024)S(1)}, f32[4096]{0:T(1024)}, u32[]{:S(2)}) copy-start(f32[4096]{0:T(1024)} %param.17) | copy-start | bytes 49156
  242.2 21.9 %all-to-all-start.1 = ((f32[128,1,128]{2,1,0:T(1,128)}), f32[128,1,128]{2,1,0:T(1,128)S(1)}, u32[]{:S(2)}, u32[]{:S(2)}) async-start(f32[128,1,128]{2,1,0:T(1,128)} %reshape.161), calls=%async_computation.1 | async-start | bytes 131072 | tf_op jit(solution)/shard_map/all_to_all | solution.py:27
  265.8 4.1 copy-start.7
  269.9 20.2 %copy-start.3 = (bf16[32,512]{1,0:T(8,128)(2,1)S(1)}, bf16[32,512]{1,0:T(8,128)(2,1)}, u32[]{:S(2)}) copy-start(bf16[32,512]{1,0:T(8,128)(2,1)} %param.20) | copy-start | bytes 98308
  271.8 17.3 %all-to-all-start.3 = ((f32[128,1,128]{2,1,0:T(1,128)}), f32[128,1,128]{2,1,0:T(1,128)S(1)}, u32[]{:S(2)}, u32[]{:S(2)}) async-start(f32[128,1,128]{2,1,0:T(1,128)} %reshape.163), calls=%async_computation.3 | async-start | bytes 131072 | tf_op jit(solution)/shard_map/all_to_all | solution.py:27
  277.6 522.7 %reduce-scatter.2.cloned.1.call-start = ((), (), s32[]{:S(2)}) async-start(), calls=%async_computation.8 | async-start | bytes 81920 | tf_op jit(solution)/shard_map/reduce_scatter | solution.py:126
  846.0 2.2 copy-start.1
  850.8 2.6 copy-start.4
Sparse Core Ops, SparseCore 0:
  10.1 33.8 all-gather.3
  47.2 181.7 all-gather.5
  778.4 21.9 reduce-scatter.1
